TPU v7x, 32 devices: a whole 2x2x4 slice. The times are simulated.
32 devices in a mesh: dp: 2 (over core), row: 4 (over y, x), col: 4 (over z).
Axes of the slice: x: 2, y: 2, z: 4, core: 2. Of those that a mesh axis runs over, the one named last changes fastest.
Arguments:
- tokens: bfloat16 [768, 32768], P('col', ('dp', 'row')), may hold values from -6 to 6
- w_qkv: bfloat16 [768, 3, 768], P(('dp', 'row'), None, 'col'), may hold values from -0.3125 to 0.3125
- bias_qv: float32 [2, 768], P(None, 'col'), may hold values from -3 to 3
- w_attn_out: bfloat16 [768, 768], P(('dp', 'row'), 'col'), may hold values from -0.875 to 0.875
- bias_attn_out: float32 [768], P('col'), may hold values from -3 to 3
- w_in: bfloat16 [768, 3072], P(('dp', 'row'), 'col'), may hold values from -0.21875 to 0.21875
- bias_in: float32 [3072], P('col'), may hold values from -3 to 3
- w_out: bfloat16 [768, 3072], P(('dp', 'row'), 'col'), may hold values from -0.21875 to 0.21875
- bias_out: float32 [768], P('col'), may hold values from -3 to 3
- norm_gains: float32 [2, 768], P(None, 'col'), may hold values from 0.5 to 1.5
- norm_biases: float32 [2, 768], P(None, 'col'), may hold values from -3 to 3
- seq_lengths: int32 [32], P(('dp', 'row')), may hold values from 256 to 1024, as said below
- seq_offsets: int32 [32], P(('dp', 'row')), may hold values from 0 to 768, as said below
- cotangent: bfloat16 [768, 32768], P('col', ('dp', 'row')), may hold values from -6 to 6
Outputs:
- activations: float32 [768, 32768], P('col', ('dp', 'row'))
- token_grad: float32 [768, 32768], P('col', ('dp', 'row'))
- grad_qkv: float32 [768, 3, 768], P(('dp', 'row'), None, 'col')
- grad_bias_qv: float32 [2, 768], P(None, 'col')
- grad_attn_out: float32 [768, 768], P(('dp', 'row'), 'col')
- grad_bias_attn_out: float32 [768], P('col')
- grad_in: float32 [768, 3072], P(('dp', 'row'), 'col')
- grad_bias_in: float32 [3072], P('col')
- grad_out: float32 [768, 3072], P(('dp', 'row'), 'col')
- grad_bias_out: float32 [768], P('col')
- grad_norm_gains: float32 [2, 768], P(None, 'col')
- grad_norm_biases: float32 [2, 768], P(None, 'col')
Inputs may be any that keep to these rules, and one draw needn't show every extreme that they name: seq_lengths[j] is the length of the one sequence of window j (tokens j * 1024 to (j + 1) * 1024 - 1); 1024 and 256 occur in every draw. seq_offsets[j] + seq_lengths[j] <= 1024: the sequence lies inside its window, the rest of the window is padding.
All inputs are finite; a program needn't handle non-finite values.
Results may differ from a plain program's by a relative error of at most 0.014.
The roundings to bfloat16 on the way count: a program that leaves them out, or rounds other values in their place, can miss the bound.
Values may be sent and summed in bfloat16 or wider, within the bound.
A program may use at most 192 MiB of HBM per device.

v0:
```python
import jax
import jax.numpy as jnp
from jax import lax
from jax.sharding import PartitionSpec as P

D = 768
HEAD_DIM = 64
PACK = 2048
SEQ_MAX = 1024
QBLOCK = 512
EPSILON = 1e-12


def row_totals(first, second):
    return lax.psum((jnp.sum(first, axis=1), jnp.sum(second, axis=1)), "col")


def norm_forward(values, gain_row, shift_row):
    totals = row_totals(values, values * values)
    average = totals[0] / D
    spread = totals[1] / D - average * average
    inverse = lax.rsqrt(spread + EPSILON)
    scaled = (values - average[:, None]) * inverse[:, None]
    return (scaled * gain_row + shift_row, scaled, inverse)


def norm_backward(upstream, scaled, inverse, gain_row):
    weighted = upstream * gain_row
    totals = row_totals(weighted, weighted * scaled)
    return inverse[:, None] * (
        weighted - (totals[0] / D)[:, None] - scaled * (totals[1] / D)[:, None]
    )


def input_total(partial_rows):
    return lax.psum_scatter(partial_rows, "col", scatter_dimension=1, tiled=True)


def grad_rows(values):
    return lax.all_gather(values, "col", axis=1, tiled=True)


def masked_scores(query_block, key_rows, live_mask, first_row):
    scores = jnp.einsum(
        "wqhe,wkhe->whqk", query_block, key_rows, preferred_element_type=jnp.float32
    ) * HEAD_DIM ** (-0.5)
    allowed = live_mask[:, first_row : first_row + QBLOCK, None] == live_mask[:, None, :]
    return jnp.where(allowed[:, None], scores, -1e30)


def attend_forward(queries, key_rows, values, live_mask):
    outputs = []
    log_totals = []
    for first_row in range(0, SEQ_MAX, QBLOCK):
        scores = masked_scores(
            queries[:, first_row : first_row + QBLOCK], key_rows, live_mask, first_row
        )
        largest = jnp.max(scores, axis=-1, keepdims=True)
        exponent = jnp.exp(scores - largest)
        row_total = jnp.sum(exponent, axis=-1, keepdims=True)
        soft_weights = (exponent / row_total).astype(jnp.bfloat16)
        outputs.append(
            jnp.einsum("whqk,wkhe->wqhe", soft_weights, values, preferred_element_type=jnp.float32)
        )
        log_totals.append(largest + jnp.log(row_total))
    return (jnp.concatenate(outputs, axis=1), log_totals)


def attend_backward(queries, key_rows, values, live_mask, log_totals, d_attended):
    score_scale = HEAD_DIM ** (-0.5)
    grad_keys = jnp.zeros(key_rows.shape, jnp.float32)
    grad_values = jnp.zeros(values.shape, jnp.float32)
    grad_queries = []
    for block_index in range(SEQ_MAX // QBLOCK):
        first_row = block_index * QBLOCK
        query_block = queries[:, first_row : first_row + QBLOCK]
        grad_block = d_attended[:, first_row : first_row + QBLOCK]
        scores = masked_scores(query_block, key_rows, live_mask, first_row)
        soft_weights = jnp.exp(scores - log_totals[block_index])
        d_weights = jnp.einsum(
            "wqhe,wkhe->whqk", grad_block, values, preferred_element_type=jnp.float32
        )
        centre = jnp.sum(soft_weights * d_weights, axis=-1, keepdims=True)
        d_scores = (soft_weights * (d_weights - centre)).astype(jnp.bfloat16)
        grad_queries.append(
            jnp.einsum("whqk,wkhe->wqhe", d_scores, key_rows, preferred_element_type=jnp.float32)
            * score_scale
        )
        grad_keys = (
            grad_keys
            + jnp.einsum(
                "whqk,wqhe->wkhe", d_scores, query_block, preferred_element_type=jnp.float32
            )
            * score_scale
        )
        grad_values = grad_values + jnp.einsum(
            "whqk,wqhe->wkhe",
            soft_weights.astype(jnp.bfloat16),
            grad_block,
            preferred_element_type=jnp.float32,
        )
    return (jnp.concatenate(grad_queries, axis=1), grad_keys, grad_values)


def contract_last(left, right):
    return lax.dot_general(
        left, right, (((1,), (1,)), ((), ())), preferred_element_type=jnp.float32
    )


def contract_first(left, right):
    return lax.dot_general(
        left, right, (((0,), (0,)), ((), ())), preferred_element_type=jnp.float32
    )


def local(
    tokens,
    w_qkv,
    bias_qv,
    w_attn_out,
    bias_attn_out,
    w_in,
    bias_in,
    w_out,
    bias_out,
    norm_gains,
    norm_biases,
    seq_lengths,
    seq_offsets,
    cotangent,
):
    part_width = tokens.shape[0]
    head_width = w_qkv.shape[2]
    head_count = head_width // HEAD_DIM
    micro_count = tokens.shape[1] // PACK
    windows = PACK // SEQ_MAX
    window_shape = (windows, SEQ_MAX, head_count, HEAD_DIM)
    places = jnp.arange(SEQ_MAX, dtype=jnp.int32)
    weight_zero = (
        jnp.zeros(w_qkv.shape, jnp.float32),
        jnp.zeros(w_attn_out.shape, jnp.float32),
        jnp.zeros(w_in.shape, jnp.float32),
        jnp.zeros(w_out.shape, jnp.float32),
    )
    small_zero = (
        jnp.zeros(bias_qv.shape, jnp.float32),
        jnp.zeros(bias_attn_out.shape, jnp.float32),
        jnp.zeros(bias_in.shape, jnp.float32),
        jnp.zeros(bias_out.shape, jnp.float32),
        jnp.zeros(norm_gains.shape, jnp.float32),
        jnp.zeros(norm_biases.shape, jnp.float32),
    )

    def micro_step(carried, inputs):
        token_cols, upstream_cols, lengths, offsets = inputs
        weight_sums, small_sums = carried
        gathered = (
            lax.all_gather(w_qkv, ("dp", "row"), axis=0, tiled=True),
            lax.all_gather(w_attn_out, ("dp", "row"), axis=0, tiled=True),
            lax.all_gather(w_in, ("dp", "row"), axis=0, tiled=True),
            lax.all_gather(w_out, ("dp", "row"), axis=0, tiled=True),
        )
        full_qkv, full_attn_out, full_in, full_out = gathered
        live_mask = (places[None, :] >= offsets[:, None]) & (
            places[None, :] < offsets[:, None] + lengths[:, None]
        )
        live_rows = live_mask.reshape(PACK).astype(jnp.float32)[:, None]
        token_full_cols = lax.all_gather(token_cols, "col", axis=0, tiled=True)
        projected = jnp.einsum(
            "dt,dke->tke", token_full_cols, full_qkv, preferred_element_type=jnp.float32
        )
        queries = (projected[:, 0] + bias_qv[0]).astype(jnp.bfloat16).reshape(window_shape)
        key_rows = projected[:, 1].astype(jnp.bfloat16).reshape(window_shape)
        values = (projected[:, 2] + bias_qv[1]).astype(jnp.bfloat16).reshape(window_shape)
        attended, log_totals = attend_forward(queries, key_rows, values, live_mask)
        attended = attended.reshape(PACK, head_width).astype(jnp.bfloat16)
        branch = lax.psum_scatter(
            contract_last(attended, full_attn_out), "col", scatter_dimension=1, tiled=True
        )
        first_sum = token_cols.astype(jnp.float32).T + branch + bias_attn_out
        normed, scaled_one, inverse_one = norm_forward(first_sum, norm_gains[0], norm_biases[0])
        normed_full = lax.all_gather(normed.astype(jnp.bfloat16), "col", axis=1, tiled=True)
        hidden = jnp.dot(normed_full, full_in, preferred_element_type=jnp.float32) + bias_in
        active_low = jax.nn.gelu(hidden, approximate=False).astype(jnp.bfloat16)
        second = lax.psum_scatter(
            contract_last(active_low, full_out), "col", scatter_dimension=1, tiled=True
        )
        second_sum = normed + second + bias_out
        result, scaled_two, inverse_two = norm_forward(second_sum, norm_gains[1], norm_biases[1])
        activations = (result * live_rows).T
        regathered = (
            lax.all_gather(w_qkv, ("dp", "row"), axis=0, tiled=True),
            lax.all_gather(w_attn_out, ("dp", "row"), axis=0, tiled=True),
            lax.all_gather(w_in, ("dp", "row"), axis=0, tiled=True),
            lax.all_gather(w_out, ("dp", "row"), axis=0, tiled=True),
        )
        back_qkv, back_attn_out, back_in, back_out = regathered
        upstream = upstream_cols.astype(jnp.float32).T * live_rows
        gain_two = jnp.sum(upstream * scaled_two, axis=0)
        shift_two = jnp.sum(upstream, axis=0)
        d_second = norm_backward(upstream, scaled_two, inverse_two, norm_gains[1])
        bias_out_grad = jnp.sum(d_second, axis=0)
        d_second_full = grad_rows(d_second.astype(jnp.bfloat16))
        out_grad = contract_first(d_second_full, active_low)
        d_active = jnp.dot(d_second_full, back_out, preferred_element_type=jnp.float32)
        gelu_pull = jax.vjp(lambda pre_act: jax.nn.gelu(pre_act, approximate=False), hidden)[1]
        d_hidden = gelu_pull(d_active)[0]
        bias_in_grad = jnp.sum(d_hidden, axis=0)
        d_hidden_low = d_hidden.astype(jnp.bfloat16)
        in_grad = contract_first(normed_full, d_hidden_low)
        d_normed = d_second + input_total(contract_last(d_hidden_low, back_in))
        gain_one = jnp.sum(d_normed * scaled_one, axis=0)
        shift_one = jnp.sum(d_normed, axis=0)
        d_first = norm_backward(d_normed, scaled_one, inverse_one, norm_gains[0])
        bias_attn_grad = jnp.sum(d_first, axis=0)
        d_first_full = grad_rows(d_first.astype(jnp.bfloat16))
        attn_out_grad = contract_first(d_first_full, attended)
        d_attended = jnp.dot(
            d_first_full, back_attn_out, preferred_element_type=jnp.float32
        ).astype(jnp.bfloat16)
        grad_q, grad_k, grad_v = attend_backward(
            queries, key_rows, values, live_mask, log_totals, d_attended.reshape(window_shape)
        )
        grad_q = grad_q.reshape(PACK, head_width)
        grad_k = grad_k.reshape(PACK, head_width)
        grad_v = grad_v.reshape(PACK, head_width)
        qv_grad = jnp.stack([jnp.sum(grad_q, axis=0), jnp.sum(grad_v, axis=0)])
        d_projected = jnp.stack([grad_q, grad_k, grad_v], axis=1).astype(jnp.bfloat16)
        qkv_grad = jnp.einsum(
            "dt,tke->dke", token_full_cols, d_projected, preferred_element_type=jnp.float32
        )
        token_grad = (
            d_first
            + input_total(
                jnp.einsum("tke,dke->td", d_projected, back_qkv, preferred_element_type=jnp.float32)
            )
        ).T
        summed = (
            lax.psum_scatter(qkv_grad, ("dp", "row"), scatter_dimension=0, tiled=True),
            lax.psum_scatter(attn_out_grad, ("dp", "row"), scatter_dimension=0, tiled=True),
            lax.psum_scatter(in_grad, ("dp", "row"), scatter_dimension=0, tiled=True),
            lax.psum_scatter(out_grad, ("dp", "row"), scatter_dimension=0, tiled=True),
        )
        weight_sums = jax.tree.map(jnp.add, weight_sums, summed)
        small_terms = (
            qv_grad,
            bias_attn_grad,
            bias_in_grad,
            bias_out_grad,
            jnp.stack([gain_one, gain_two]),
            jnp.stack([shift_one, shift_two]),
        )
        small_sums = jax.tree.map(jnp.add, small_sums, small_terms)
        return ((weight_sums, small_sums), (activations, token_grad))

    token_blocks = tokens.reshape(part_width, micro_count, PACK).transpose(1, 0, 2)
    upstream_blocks = cotangent.reshape(part_width, micro_count, PACK).transpose(1, 0, 2)
    inputs = (
        token_blocks,
        upstream_blocks,
        seq_lengths.reshape(micro_count, windows),
        seq_offsets.reshape(micro_count, windows),
    )
    finals, stacked = lax.scan(micro_step, (weight_zero, small_zero), inputs)
    weight_sums, small_sums = finals
    small_sums = lax.psum(
        (small_sums[0], small_sums[1], small_sums[2], small_sums[3], small_sums[4], small_sums[5]),
        ("dp", "row"),
    )
    activations = stacked[0].transpose(1, 0, 2).reshape(part_width, micro_count * PACK)
    token_grads = stacked[1].transpose(1, 0, 2).reshape(part_width, micro_count * PACK)
    return (
        activations,
        token_grads,
        weight_sums[0],
        small_sums[0],
        weight_sums[1],
        small_sums[1],
        weight_sums[2],
        small_sums[2],
        weight_sums[3],
        small_sums[3],
        small_sums[4],
        small_sums[5],
    )


def solution(mesh):
    return jax.shard_map(
        local,
        mesh=mesh,
        in_specs=(
            P("col", ("dp", "row")),
            P(("dp", "row"), None, "col"),
            P(None, "col"),
            P(("dp", "row"), "col"),
            P("col"),
            P(("dp", "row"), "col"),
            P("col"),
            P(("dp", "row"), "col"),
            P("col"),
            P(None, "col"),
            P(None, "col"),
            P(("dp", "row")),
            P(("dp", "row")),
            P("col", ("dp", "row")),
        ),
        out_specs=(
            P("col", ("dp", "row")),
            P("col", ("dp", "row")),
            P(("dp", "row"), None, "col"),
            P(None, "col"),
            P(("dp", "row"), "col"),
            P("col"),
            P(("dp", "row"), "col"),
            P("col"),
            P(("dp", "row"), "col"),
            P("col"),
            P(None, "col"),
            P(None, "col"),
        ),
        check_vma=False,
    )
```

profile of v0, /device:TPU:1, one launch (start us, length us, event | category | flops | bytes accessed | tf_op | source)
XLA Modules:
  0.0 2196.4 jit_solution(1545050451613228207)
XLA Ops:
  19.6 2135.8 %while.34 = (s32[]{:T(128)}, f32[96,3,192]{2,0,1:T(8,128)}, f32[96,192]{1,0:T(8,128)}, f32[96,768]{1,0:T(8,128)}, f32[96,768]{1,0:T(8,128)}, /*index=5*/f32[2,19...) while((s32[]{:T(128)}, f32[96,3,192]{2,0,1:T(8,128)}, ...), condition=%wide.region_41.42_spmd.clone.clone, body=%wide.region_0.41_spmd.clone.clone.sunk | while | flops 26853322752 | bytes 1020480256 | solution.py:265
  21.6 35.5 %all_gather.50 = bf16[768,3,192]{2,1,0:T(4,128)(2,1)S(1)} all-gather(bf16[96,3,192]{2,1,0:T(4,128)(2,1)} %get-tuple-element.915), channel_id=1, replica_groups=mesh['dp'=2,'row'=4,'col'=4] {'dp','row'}, dimensions={0}, use_global_device_ids=true | all-gather | bytes 995328 | tf_op jit(solution)/shard_map/while/body/eval_jaxpr/all_gather | solution.py:159
  59.3 24.1 %all_gather.51 = bf16[768,192]{1,0:T(8,128)(2,1)S(1)} all-gather(bf16[96,192]{1,0:T(8,128)(2,1)S(1)} %copy-done.45), channel_id=1, replica_groups=mesh['dp'=2,'row'=4,'col'=4] {'dp','row'}, dimensions={0}, use_global_device_ids=true | all-gather | bytes 331776 | tf_op jit(solution)/shard_map/while/body/eval_jaxpr/all_gather | solution.py:160
  130.9 106.3 %reduce-scatter.9.cloned.1.call-done = f32[2048,192]{0,1:T(8,128)} async-done(((f32[2048,768]{0,1:T(8,128)}), f32[2048,192]{0,1:T(8,128)}) %reduce-scatter.9.cloned.1.call-update) | async-done | bytes 1572880 | tf_op jit(solution)/shard_map/while/body/eval_jaxpr/reduce_scatter | solution.py:178
  239.0 14.4 all-reduce.9
  255.9 8.0 all-gather.15.cloned.1.call-done
  263.9 64.9 %all-gather.13.cloned.1.call-done = bf16[2048,768]{0,1:T(8,128)(2,1)} async-done(((bf16[2048,192]{0,1:T(8,128)(2,1)}), bf16[2048,768]{0,1:T(8,128)(2,1)}) %all-gather.13.cloned.1.call-update) | async-done | bytes 3145744 | tf_op jit(solution)/shard_map/while/body/eval_jaxpr/all_gather | solution.py:183
  328.8 19.3 multiply_convert_fusion.7
  353.7 7.5 fusion.247
  361.9 109.8 %reduce-scatter.11.cloned.1.call-done = f32[2048,192]{0,1:T(8,128)} async-done(((f32[2048,768]{0,1:T(8,128)}), f32[2048,192]{0,1:T(8,128)}) %reduce-scatter.11.cloned.1.call-update) | async-done | bytes 1572880 | tf_op jit(solution)/shard_map/while/body/eval_jaxpr/reduce_scatter | solution.py:186
  474.3 15.8 all-reduce.10
  493.7 13.2 all-reduce.11
  511.5 69.3 %all-gather.19.cloned.1.call-done = bf16[2048,768]{0,1:T(8,128)(2,1)} async-done(((bf16[2048,192]{0,1:T(8,128)(2,1)}), bf16[2048,768]{0,1:T(8,128)(2,1)}) %all-gather.19.cloned.1.call-update) | async-done | bytes 3145744 | tf_op jit(solution)/shard_map/while/body/eval_jaxpr/all_gather | solution.py:40
  580.7 11.4 fusion.250
  598.3 109.6 %reduce-scatter.13.cloned.1.call-done = f32[2048,192]{0,1:T(8,128)} async-done(((f32[2048,768]{0,1:T(8,128)}), f32[2048,192]{0,1:T(8,128)}) %reduce-scatter.13.cloned.1.call-update) | async-done | bytes 1572880 | tf_op jit(solution)/shard_map/while/body/eval_jaxpr/reduce_scatter | solution.py:36
  712.8 15.1 all-reduce.12
  732.7 6.8 fusion.262
  739.7 7.1 fusion.263
  747.3 50.7 %all-gather.21.cloned.1.call-done = bf16[2048,768]{0,1:T(8,128)(2,1)} async-done(((bf16[2048,192]{0,1:T(8,128)(2,1)}), bf16[2048,768]{0,1:T(8,128)(2,1)}) %all-gather.21.cloned.1.call-update) | async-done | bytes 3145744 | tf_op jit(solution)/shard_map/while/body/eval_jaxpr/all_gather | solution.py:40
  808.0 10.3 multiply_reduce_fusion.13
  829.9 9.8 multiply_convert_fusion.9
  898.4 27.1 %reduce-scatter.17.cloned.1.call-done = f32[96,192]{1,0:T(8,128)} async-done(((f32[768,192]{1,0:T(8,128)}), f32[96,192]{1,0:T(8,128)}) %reduce-scatter.17.cloned.1.call-update) | async-done | bytes 73744 | tf_op jit(solution)/shard_map/while/body/eval_jaxpr/reduce_scatter | solution.py:241
  926.4 45.2 %reduce-scatter.15.cloned.1.call-done = f32[96,3,192]{2,0,1:T(8,128)} async-done(((f32[768,3,192]{2,0,1:T(8,128)}), f32[96,3,192]{2,0,1:T(8,128)}) %reduce-scatter.15.cloned.1.call-update) | async-done | bytes 221200 | tf_op jit(solution)/shard_map/while/body/eval_jaxpr/reduce_scatter | solution.py:240
  973.3 111.4 %reduce-scatter.23.cloned.1.call-done = f32[2048,192]{0,1:T(8,128)} async-done(((f32[2048,768]{0,1:T(8,128)}), f32[2048,192]{0,1:T(8,128)}) %reduce-scatter.23.cloned.1.call-update) | async-done | bytes 1572880 | tf_op jit(solution)/shard_map/while/body/eval_jaxpr/reduce_scatter | solution.py:36
  1089.9 34.6 %all_gather.50 = bf16[768,3,192]{2,1,0:T(4,128)(2,1)S(1)} all-gather(bf16[96,3,192]{2,1,0:T(4,128)(2,1)} %get-tuple-element.915), channel_id=1, replica_groups=mesh['dp'=2,'row'=4,'col'=4] {'dp','row'}, dimensions={0}, use_global_device_ids=true | all-gather | bytes 995328 | tf_op jit(solution)/shard_map/while/body/eval_jaxpr/all_gather | solution.py:159
  1126.6 24.2 %all_gather.51 = bf16[768,192]{1,0:T(8,128)(2,1)S(1)} all-gather(bf16[96,192]{1,0:T(8,128)(2,1)S(1)} %copy-done.45), channel_id=1, replica_groups=mesh['dp'=2,'row'=4,'col'=4] {'dp','row'}, dimensions={0}, use_global_device_ids=true | all-gather | bytes 331776 | tf_op jit(solution)/shard_map/while/body/eval_jaxpr/all_gather | solution.py:160
  1196.8 106.4 %reduce-scatter.9.cloned.1.call-done = f32[2048,192]{0,1:T(8,128)} async-done(((f32[2048,768]{0,1:T(8,128)}), f32[2048,192]{0,1:T(8,128)}) %reduce-scatter.9.cloned.1.call-update) | async-done | bytes 1572880 | tf_op jit(solution)/shard_map/while/body/eval_jaxpr/reduce_scatter | solution.py:178
  1305.0 14.5 all-reduce.9
  1322.2 7.6 all-gather.15.cloned.1.call-done
  1329.8 64.9 %all-gather.13.cloned.1.call-done = bf16[2048,768]{0,1:T(8,128)(2,1)} async-done(((bf16[2048,192]{0,1:T(8,128)(2,1)}), bf16[2048,768]{0,1:T(8,128)(2,1)}) %all-gather.13.cloned.1.call-update) | async-done | bytes 3145744 | tf_op jit(solution)/shard_map/while/body/eval_jaxpr/all_gather | solution.py:183
  1394.7 19.3 multiply_convert_fusion.7
  1419.8 7.5 fusion.247
  1427.9 109.8 %reduce-scatter.11.cloned.1.call-done = f32[2048,192]{0,1:T(8,128)} async-done(((f32[2048,768]{0,1:T(8,128)}), f32[2048,192]{0,1:T(8,128)}) %reduce-scatter.11.cloned.1.call-update) | async-done | bytes 1572880 | tf_op jit(solution)/shard_map/while/body/eval_jaxpr/reduce_scatter | solution.py:186
  1540.4 16.0 all-reduce.10
  1559.9 13.2 all-reduce.11
  1577.8 69.3 %all-gather.19.cloned.1.call-done = bf16[2048,768]{0,1:T(8,128)(2,1)} async-done(((bf16[2048,192]{0,1:T(8,128)(2,1)}), bf16[2048,768]{0,1:T(8,128)(2,1)}) %all-gather.19.cloned.1.call-update) | async-done | bytes 3145744 | tf_op jit(solution)/shard_map/while/body/eval_jaxpr/all_gather | solution.py:40
  1647.0 11.4 fusion.250
  1664.6 109.6 %reduce-scatter.13.cloned.1.call-done = f32[2048,192]{0,1:T(8,128)} async-done(((f32[2048,768]{0,1:T(8,128)}), f32[2048,192]{0,1:T(8,128)}) %reduce-scatter.13.cloned.1.call-update) | async-done | bytes 1572880 | tf_op jit(solution)/shard_map/while/body/eval_jaxpr/reduce_scatter | solution.py:36
  1779.1 15.1 all-reduce.12
  1798.9 6.8 fusion.262
  1805.9 7.1 fusion.263
  1813.3 51.0 %all-gather.21.cloned.1.call-done = bf16[2048,768]{0,1:T(8,128)(2,1)} async-done(((bf16[2048,192]{0,1:T(8,128)(2,1)}), bf16[2048,768]{0,1:T(8,128)(2,1)}) %all-gather.21.cloned.1.call-update) | async-done | bytes 3145744 | tf_op jit(solution)/shard_map/while/body/eval_jaxpr/all_gather | solution.py:40
  1874.3 10.3 multiply_reduce_fusion.13
  1896.2 9.8 multiply_convert_fusion.9
  1965.9 25.9 %reduce-scatter.17.cloned.1.call-done = f32[96,192]{1,0:T(8,128)} async-done(((f32[768,192]{1,0:T(8,128)}), f32[96,192]{1,0:T(8,128)}) %reduce-scatter.17.cloned.1.call-update) | async-done | bytes 73744 | tf_op jit(solution)/shard_map/while/body/eval_jaxpr/reduce_scatter | solution.py:241
  1992.8 45.0 %reduce-scatter.15.cloned.1.call-done = f32[96,3,192]{2,0,1:T(8,128)} async-done(((f32[768,3,192]{2,0,1:T(8,128)}), f32[96,3,192]{2,0,1:T(8,128)}) %reduce-scatter.15.cloned.1.call-update) | async-done | bytes 221200 | tf_op jit(solution)/shard_map/while/body/eval_jaxpr/reduce_scatter | solution.py:240
  2039.6 111.4 %reduce-scatter.23.cloned.1.call-done = f32[2048,192]{0,1:T(8,128)} async-done(((f32[2048,768]{0,1:T(8,128)}), f32[2048,192]{0,1:T(8,128)}) %reduce-scatter.23.cloned.1.call-update) | async-done | bytes 1572880 | tf_op jit(solution)/shard_map/while/body/eval_jaxpr/reduce_scatter | solution.py:36
  2159.5 27.9 %all-reduce.4 = (f32[2,192]{1,0:T(2,128)}, f32[192]{0:T(256)}, f32[768]{0:T(1024)}, f32[192]{0:T(256)}, f32[2,192]{1,0:T(2,128)}, /*index=5*/f32[2,192]{1,0:T(2,128)}) all-reduce(f32[2,192]{1,0:T(2,128)S(1)} %copy-done.54, f32[192]{0:T(256)S(1)} %copy-done.56, ...), channel_id=1, replica_groups=mesh['dp'=2,'row'=4,'col'=4] {'dp','row'}, use_global_device_ids=true, to_apply=%region_42.43 | all-reduce | flops 2304 | bytes 18432 | tf_op jit(solution)/shard_map/psum | solution.py:267
  (523 shorter events, 366.9 us)
Async XLA Ops:
  19.6 68.3 %all-gather.11.cloned.1.call-start = ((), (), s32[]{:S(2)}) async-start(), calls=%async_computation.8 | async-start | bytes 3932160 | tf_op jit(solution)/shard_map/while/body/eval_jaxpr/all_gather | solution.py:169
  19.6 39.7 %copy-start.45 = (bf16[96,192]{1,0:T(8,128)(2,1)S(1)}, bf16[96,192]{1,0:T(8,128)(2,1)}, u32[]{:S(2)}) copy-start(bf16[96,192]{1,0:T(8,128)(2,1)} %get-tuple-element.919) | copy-start | bytes 110596 | tf_op jit(solution)/shard_map/while
  20.7 216.5 %reduce-scatter.9.cloned.1.call-start = ((), (), s32[]{:S(2)}) async-start(), calls=%async_computation.9 | async-start | bytes 7864320 | tf_op jit(solution)/shard_map/while/body/eval_jaxpr/reduce_scatter | solution.py:178
  127.4 109.7 %copy-start.20 = (bf16[2,192,2048]{2,1,0:T(8,128)(2,1)S(1)}, bf16[2,192,2048]{2,1,0:T(8,128)(2,1)}, u32[]{:S(2)}) copy-start(bf16[2,192,2048]{2,1,0:T(8,128)(2,1)} %copy-done.19) | copy-start | bytes 4718596 | tf_op jit(solution)/shard_map/while
  127.4 136.5 %all-gather.15.cloned.1.call-start = ((), (), s32[]{:S(2)}) async-start(), calls=%async_computation.11 | async-start | bytes 1327104 | tf_op jit(solution)/shard_map/while/body/eval_jaxpr/all_gather | solution.py:161
  128.2 200.6 %all-gather.13.cloned.1.call-start = ((), (), s32[]{:S(2)}) async-start(), calls=%async_computation.10 | async-start | bytes 3932160 | tf_op jit(solution)/shard_map/while/body/eval_jaxpr/all_gather | solution.py:183
  238.9 89.9 %copy-start.58 = (f32[768]{0:T(1024)S(1)}, f32[768]{0:T(1024)}, u32[]{:S(2)}) copy-start(f32[768]{0:T(1024)} %get-tuple-element.924) | copy-start | bytes 9220 | tf_op jit(solution)/shard_map/while
  253.4 94.7 %copy-start.31 = (f32[2048]{0:T(1024)}, f32[2048]{0:T(1024)S(1)}, u32[]{:S(2)}) copy-start(f32[2048]{0:T(1024)S(1)} %get-tuple-element.795) | copy-start | bytes 24580 | tf_op jit(solution)/shard_map/while
  253.4 218.3 %copy-start.30 = (f32[2048]{0:T(1024)}, f32[2048]{0:T(1024)S(1)}, u32[]{:S(2)}) copy-start(f32[2048]{0:T(1024)S(1)} %get-tuple-element.796) | copy-start | bytes 24580 | tf_op jit(solution)/shard_map/while
  255.3 98.4 %all-gather.17.cloned.1.call-start = ((), (), s32[]{:S(2)}) async-start(), calls=%async_computation.12 | async-start | bytes 1327104 | tf_op jit(solution)/shard_map/while/body/eval_jaxpr/all_gather | solution.py:162
  255.9 215.8 %reduce-scatter.11.cloned.1.call-start = ((), (), s32[]{:S(2)}) async-start(), calls=%async_computation.13 | async-start | bytes 7864320 | tf_op jit(solution)/shard_map/while/body/eval_jaxpr/reduce_scatter | solution.py:186
  361.2 219.5 %all-gather.19.cloned.1.call-start = ((), (), s32[]{:S(2)}) async-start(), calls=%async_computation.14 | async-start | bytes 3932160 | tf_op jit(solution)/shard_map/while/body/eval_jaxpr/all_gather | solution.py:40
  474.3 233.6 %copy-start.4 = (f32[2048,192]{0,1:T(8,128)}, f32[2048,192]{0,1:T(8,128)S(1)}, u32[]{:S(2)}) copy-start(f32[2048,192]{0,1:T(8,128)S(1)} %get-tuple-element.798) | copy-start | bytes 4718596 | tf_op jit(solution)/shard_map/while
  511.4 196.5 %reduce-scatter.13.cloned.1.call-start = ((), (), s32[]{:S(2)}) async-start(), calls=%async_computation.15 | async-start | bytes 7864320 | tf_op jit(solution)/shard_map/while/body/eval_jaxpr/reduce_scatter | solution.py:36
  598.3 199.7 %all-gather.21.cloned.1.call-start = ((), (), s32[]{:S(2)}) async-start(), calls=%async_computation.16 | async-start | bytes 3932160 | tf_op jit(solution)/shard_map/while/body/eval_jaxpr/all_gather | solution.py:40
  732.6 156.9 %reduce-scatter.19.cloned.1.call-start = ((), (), s32[]{:S(2)}) async-start(), calls=%async_computation.19 | async-start | bytes 2654208 | tf_op jit(solution)/shard_map/while/body/eval_jaxpr/reduce_scatter | solution.py:242
  739.5 151.7 %reduce-scatter.21.cloned.1.call-start = ((), (), s32[]{:S(2)}) async-start(), calls=%async_computation.20 | async-start | bytes 2654208 | tf_op jit(solution)/shard_map/while/body/eval_jaxpr/reduce_scatter | solution.py:243
  746.8 178.7 %reduce-scatter.17.cloned.1.call-start = ((), (), s32[]{:S(2)}) async-start(), calls=%async_computation.18 | async-start | bytes 884736 | tf_op jit(solution)/shard_map/while/body/eval_jaxpr/reduce_scatter | solution.py:241
  870.9 100.7 %reduce-scatter.15.cloned.1.call-start = ((), (), s32[]{:S(2)}) async-start(), calls=%async_computation.17 | async-start | bytes 2654208 | tf_op jit(solution)/shard_map/while/body/eval_jaxpr/reduce_scatter | solution.py:240
  879.6 205.0 %reduce-scatter.23.cloned.1.call-start = ((), (), s32[]{:S(2)}) async-start(), calls=%async_computation.21 | async-start | bytes 7864320 | tf_op jit(solution)/shard_map/while/body/eval_jaxpr/reduce_scatter | solution.py:36
  886.7 198.0 %copy-start.7 = (f32[2048,192]{0,1:T(8,128)S(1)}, f32[2048,192]{0,1:T(8,128)}, u32[]{:S(2)}) copy-start(f32[2048,192]{0,1:T(8,128)} %copy-done.6) | copy-start | bytes 4718596 | tf_op jit(solution)/shard_map/while
  892.3 195.1 %copy-start.26 = (f32[96,768]{1,0:T(8,128)}, f32[96,768]{1,0:T(8,128)S(1)}, u32[]{:S(2)}) copy-start(f32[96,768]{1,0:T(8,128)S(1)} %select_add_fusion.17) | copy-start | bytes 884740 | tf_op jit(solution)/shard_map/while
  897.6 189.8 %copy-start.21 = (bf16[2,192,2048]{2,1,0:T(8,128)(2,1)S(1)}, bf16[2,192,2048]{2,1,0:T(8,128)(2,1)}, u32[]{:S(2)}) copy-start(bf16[2,192,2048]{2,1,0:T(8,128)(2,1)} %copy-done.19) | copy-start | bytes 4718596 | tf_op jit(solution)/shard_map/while
  926.4 161.0 %copy-start.34 = (f32[96,192]{1,0:T(8,128)}, f32[96,192]{1,0:T(8,128)S(1)}, u32[]{:S(2)}) copy-start(f32[96,192]{1,0:T(8,128)S(1)} %select_add_fusion.15) | copy-start | bytes 221188 | tf_op jit(solution)/shard_map/while
  1087.8 66.5 %all-gather.11.cloned.1.call-start = ((), (), s32[]{:S(2)}) async-start(), calls=%async_computation.8 | async-start | bytes 3932160 | tf_op jit(solution)/shard_map/while/body/eval_jaxpr/all_gather | solution.py:169
  1087.9 38.7 %copy-start.45 = (bf16[96,192]{1,0:T(8,128)(2,1)S(1)}, bf16[96,192]{1,0:T(8,128)(2,1)}, u32[]{:S(2)}) copy-start(bf16[96,192]{1,0:T(8,128)(2,1)} %get-tuple-element.919) | copy-start | bytes 110596 | tf_op jit(solution)/shard_map/while
  1088.9 214.3 %reduce-scatter.9.cloned.1.call-start = ((), (), s32[]{:S(2)}) async-start(), calls=%async_computation.9 | async-start | bytes 7864320 | tf_op jit(solution)/shard_map/while/body/eval_jaxpr/reduce_scatter | solution.py:178
  1193.5 109.7 %copy-start.20 = (bf16[2,192,2048]{2,1,0:T(8,128)(2,1)S(1)}, bf16[2,192,2048]{2,1,0:T(8,128)(2,1)}, u32[]{:S(2)}) copy-start(bf16[2,192,2048]{2,1,0:T(8,128)(2,1)} %copy-done.19) | copy-start | bytes 4718596 | tf_op jit(solution)/shard_map/while
  1193.5 136.3 %all-gather.15.cloned.1.call-start = ((), (), s32[]{:S(2)}) async-start(), calls=%async_computation.11 | async-start | bytes 1327104 | tf_op jit(solution)/shard_map/while/body/eval_jaxpr/all_gather | solution.py:161
  1194.1 200.6 %all-gather.13.cloned.1.call-start = ((), (), s32[]{:S(2)}) async-start(), calls=%async_computation.10 | async-start | bytes 3932160 | tf_op jit(solution)/shard_map/while/body/eval_jaxpr/all_gather | solution.py:183
  1305.0 89.7 %copy-start.58 = (f32[768]{0:T(1024)S(1)}, f32[768]{0:T(1024)}, u32[]{:S(2)}) copy-start(f32[768]{0:T(1024)} %get-tuple-element.924) | copy-start | bytes 9220 | tf_op jit(solution)/shard_map/while
  1319.5 94.5 %copy-start.31 = (f32[2048]{0:T(1024)}, f32[2048]{0:T(1024)S(1)}, u32[]{:S(2)}) copy-start(f32[2048]{0:T(1024)S(1)} %get-tuple-element.795) | copy-start | bytes 24580 | tf_op jit(solution)/shard_map/while
  1319.5 218.2 %copy-start.30 = (f32[2048]{0:T(1024)}, f32[2048]{0:T(1024)S(1)}, u32[]{:S(2)}) copy-start(f32[2048]{0:T(1024)S(1)} %get-tuple-element.796) | copy-start | bytes 24580 | tf_op jit(solution)/shard_map/while
  1321.4 98.4 %all-gather.17.cloned.1.call-start = ((), (), s32[]{:S(2)}) async-start(), calls=%async_computation.12 | async-start | bytes 1327104 | tf_op jit(solution)/shard_map/while/body/eval_jaxpr/all_gather | solution.py:162
  1322.1 215.6 %reduce-scatter.11.cloned.1.call-start = ((), (), s32[]{:S(2)}) async-start(), calls=%async_computation.13 | async-start | bytes 7864320 | tf_op jit(solution)/shard_map/while/body/eval_jaxpr/reduce_scatter | solution.py:186
  1427.3 219.8 %all-gather.19.cloned.1.call-start = ((), (), s32[]{:S(2)}) async-start(), calls=%async_computation.14 | async-start | bytes 3932160 | tf_op jit(solution)/shard_map/while/body/eval_jaxpr/all_gather | solution.py:40
  1540.4 233.8 %copy-start.4 = (f32[2048,192]{0,1:T(8,128)}, f32[2048,192]{0,1:T(8,128)S(1)}, u32[]{:S(2)}) copy-start(f32[2048,192]{0,1:T(8,128)S(1)} %get-tuple-element.798) | copy-start | bytes 4718596 | tf_op jit(solution)/shard_map/while
  1577.7 196.5 %reduce-scatter.13.cloned.1.call-start = ((), (), s32[]{:S(2)}) async-start(), calls=%async_computation.15 | async-start | bytes 7864320 | tf_op jit(solution)/shard_map/while/body/eval_jaxpr/reduce_scatter | solution.py:36
  1664.5 199.7 %all-gather.21.cloned.1.call-start = ((), (), s32[]{:S(2)}) async-start(), calls=%async_computation.16 | async-start | bytes 3932160 | tf_op jit(solution)/shard_map/while/body/eval_jaxpr/all_gather | solution.py:40
  1798.9 157.2 %reduce-scatter.19.cloned.1.call-start = ((), (), s32[]{:S(2)}) async-start(), calls=%async_computation.19 | async-start | bytes 2654208 | tf_op jit(solution)/shard_map/while/body/eval_jaxpr/reduce_scatter | solution.py:242
  1805.8 152.1 %reduce-scatter.21.cloned.1.call-start = ((), (), s32[]{:S(2)}) async-start(), calls=%async_computation.20 | async-start | bytes 2654208 | tf_op jit(solution)/shard_map/while/body/eval_jaxpr/reduce_scatter | solution.py:243
  1813.1 178.8 %reduce-scatter.17.cloned.1.call-start = ((), (), s32[]{:S(2)}) async-start(), calls=%async_computation.18 | async-start | bytes 884736 | tf_op jit(solution)/shard_map/while/body/eval_jaxpr/reduce_scatter | solution.py:241
  1937.2 100.6 %reduce-scatter.15.cloned.1.call-start = ((), (), s32[]{:S(2)}) async-start(), calls=%async_computation.17 | async-start | bytes 2654208 | tf_op jit(solution)/shard_map/while/body/eval_jaxpr/reduce_scatter | solution.py:240
  1946.0 205.1 %reduce-scatter.23.cloned.1.call-start = ((), (), s32[]{:S(2)}) async-start(), calls=%async_computation.21 | async-start | bytes 7864320 | tf_op jit(solution)/shard_map/while/body/eval_jaxpr/reduce_scatter | solution.py:36
  1953.2 197.9 %copy-start.7 = (f32[2048,192]{0,1:T(8,128)S(1)}, f32[2048,192]{0,1:T(8,128)}, u32[]{:S(2)}) copy-start(f32[2048,192]{0,1:T(8,128)} %copy-done.6) | copy-start | bytes 4718596 | tf_op jit(solution)/shard_map/while
  1958.9 194.9 %copy-start.26 = (f32[96,768]{1,0:T(8,128)}, f32[96,768]{1,0:T(8,128)S(1)}, u32[]{:S(2)}) copy-start(f32[96,768]{1,0:T(8,128)S(1)} %select_add_fusion.17) | copy-start | bytes 884740 | tf_op jit(solution)/shard_map/while
  1964.4 189.4 %copy-start.21 = (bf16[2,192,2048]{2,1,0:T(8,128)(2,1)S(1)}, bf16[2,192,2048]{2,1,0:T(8,128)(2,1)}, u32[]{:S(2)}) copy-start(bf16[2,192,2048]{2,1,0:T(8,128)(2,1)} %copy-done.19) | copy-start | bytes 4718596 | tf_op jit(solution)/shard_map/while
  1992.8 161.0 %copy-start.34 = (f32[96,192]{1,0:T(8,128)}, f32[96,192]{1,0:T(8,128)S(1)}, u32[]{:S(2)}) copy-start(f32[96,192]{1,0:T(8,128)S(1)} %select_add_fusion.15) | copy-start | bytes 221188 | tf_op jit(solution)/shard_map/while
  (109 other events, 798.3 us)
Sparse Core Ops, SparseCore 0:
  22.5 65.3 all-gather.10
  127.6 109.5 reduce-scatter.8
  239.0 24.8 all-gather.14
  265.9 62.8 all-gather.12
  330.5 23.1 all-gather.16
  361.3 110.3 reduce-scatter.10
  511.5 69.1 all-gather.18
  598.4 109.5 reduce-scatter.12
  732.7 65.2 all-gather.20
  801.1 40.9 reduce-scatter.18
  845.5 42.3 reduce-scatter.20
  890.9 34.5 reduce-scatter.16
  928.8 42.7 reduce-scatter.14
  973.8 110.8 reduce-scatter.22
  1090.5 63.8 all-gather.10
  1193.6 109.5 reduce-scatter.8
  1304.9 24.8 all-gather.14
  1331.8 62.8 all-gather.12
  1396.6 23.1 all-gather.16
  1427.4 110.3 reduce-scatter.10
  1577.8 69.1 all-gather.18
  1664.7 109.5 reduce-scatter.12
  1799.0 65.2 all-gather.20
  1867.4 40.9 reduce-scatter.18
  1911.8 42.3 reduce-scatter.20
  1957.2 34.5 reduce-scatter.16
  1995.1 42.7 reduce-scatter.14
  2040.1 110.8 reduce-scatter.22
where the time goes:
time: 2200 us
  waiting for transfers between devices  1420 us (65%)
  matrix products  266 us (12%)
  blocking collectives  264 us (12%)
  other arithmetic  136 us (6%)
  local copies, waits for them, and re-layouts  90.9 us (4%)
    reduce_scatter x4, waiting for transfers between devices, input_total(): lax.psum_scatter(partial_rows, 'col', scatter_dimension=1, tiled=True)  442 us
    all_gather x4, waiting for transfers between devices, grad_rows(): return lax.all_gather(values, 'col', axis=1, tiled=True)  240 us
    reduce_scatter x2, waiting for transfers between devices, micro_step(): lax.psum_scatter(contract_last(active_low, full_out), 'col', scatter_dime...  220 us
    reduce_scatter x2, waiting for transfers between devices, micro_step(): lax.psum_scatter(contract_last(attended, full_attn_out), 'col', scatter_d...  213 us
    all_gather x2, waiting for transfers between devices, micro_step(): lax.all_gather(normed.astype(jnp.bfloat16), 'col', axis=1, tiled=True)  130 us
    psum x8, blocking collectives, row_totals(): return lax.psum((jnp.sum(first, axis=1), jnp.sum(second, axis=1)), 'col')  117 us
    reduce_scatter x2, waiting for transfers between devices, micro_step(): lax.psum_scatter(qkv_grad, ('dp', 'row'), scatter_dimension=0, tiled=True)  90.2 us
    all_gather x2, blocking collectives, micro_step(): lax.all_gather(w_qkv, ('dp', 'row'), axis=0, tiled=True)  70.2 us
  transfers between devices with their start and end apart: 28, of which 24 were waited for; matrix products, arithmetic and copies ran while one was open for 13% of the time, Pallas kernels for 0%

commit v1 on v0

--- a/solution.py
+++ b/solution.py
@@ -9,6 +9,18 @@
 SEQ_MAX = 1024
 QBLOCK = 512
 EPSILON = 1e-12
+
+
+def doubled_up(value, axis, dim):
+    ways, here, step = (lax.axis_size(axis), lax.axis_index(axis), value.shape[dim])
+    line, have = (value, 1)
+    while have < ways:
+        line = jnp.concatenate(
+            [line, lax.ppermute(line, axis, [(d, (d - have) % ways) for d in range(ways)])],
+            axis=dim,
+        )
+        have = 2 * have
+    return jnp.roll(line, here * step, axis=dim)
 
 
 def row_totals(first, second):
@@ -37,7 +49,7 @@
 
 
 def grad_rows(values):
-    return lax.all_gather(values, "col", axis=1, tiled=True)
+    return doubled_up(values, "col", 1)
 
 
 def masked_scores(query_block, key_rows, live_mask, first_row):

time: 2200 us -> 2270 us (1.032)
  other arithmetic: 136 us -> 177 us
  waiting for transfers between devices: 1420 us -> 1460 us
    ppermute x0 -> x8, waiting for transfers between devices: none -> 317 us  [doubled_up(): lax.ppermute(line, axis, [(d, (d - have) % ways) for d in range(ways)])]
    all_gather x4 -> x0, waiting for transfers between devices: 240 us -> none  [grad_rows(): return lax.all_gather(values, 'col', axis=1, tiled=True)]
    concatenate x0 -> x8, other arithmetic: none -> 42 us  [the longest x4 38.9 us: doubled_up(): return jnp.roll(line, here * step, axis=dim)]
    reduce_scatter x2, waiting for transfers between devices: 53.1 us -> 15.8 us  [micro_step(): lax.psum_scatter(attn_out_grad, ('dp', 'row'), scatter_dimension=0, tiled...]
  transfers between devices with their start and end apart: 28 -> 32, of which waited for: 24 -> 28; matrix products, arithmetic and copies ran while one was open for 13% -> 14% of each run, Pallas kernels for 0% -> 0%
where the time goes in v1:
time: 2270 us
  waiting for transfers between devices  1460 us (64%)
  blocking collectives  264 us (12%)
  matrix products  250 us (11%)
  other arithmetic  177 us (8%)
  local copies, waits for them, and re-layouts  93.9 us (4%)
    reduce_scatter x4, waiting for transfers between devices, input_total(): lax.psum_scatter(partial_rows, 'col', scatter_dimension=1, tiled=True)  442 us
    ppermute x8, waiting for transfers between devices, doubled_up(): lax.ppermute(line, axis, [(d, (d - have) % ways) for d in range(ways)])  317 us
    reduce_scatter x2, waiting for transfers between devices, micro_step(): lax.psum_scatter(contract_last(active_low, full_out), 'col', scatter_dime...  220 us
    reduce_scatter x2, waiting for transfers between devices, micro_step(): lax.psum_scatter(contract_last(attended, full_attn_out), 'col', scatter_d...  213 us
    all_gather x2, waiting for transfers between devices, micro_step(): lax.all_gather(normed.astype(jnp.bfloat16), 'col', axis=1, tiled=True)  130 us
    psum x8, blocking collectives, row_totals(): return lax.psum((jnp.sum(first, axis=1), jnp.sum(second, axis=1)), 'col')  117 us
    reduce_scatter x2, waiting for transfers between devices, micro_step(): lax.psum_scatter(qkv_grad, ('dp', 'row'), scatter_dimension=0, tiled=True)  91.5 us
    all_gather x2, blocking collectives, micro_step(): lax.all_gather(w_qkv, ('dp', 'row'), axis=0, tiled=True)  70.2 us
  transfers between devices with their start and end apart: 32, of which 28 were waited for; matrix products, arithmetic and copies ran while one was open for 14% of the time, Pallas kernels for 0%

profile of v1, /device:TPU:1, one launch (start us, length us, event | category | flops | bytes accessed | tf_op | source)
XLA Modules:
  0.0 2266.0 jit_solution(16612528704623265868)
XLA Ops:
  19.7 2205.3 %while.34 = (s32[]{:T(128)}, f32[96,3,192]{2,0,1:T(8,128)}, f32[96,192]{1,0:T(8,128)}, f32[96,768]{1,0:T(8,128)}, f32[96,768]{1,0:T(8,128)}, /*index=5*/f32[2,19...) while((s32[]{:T(128)}, f32[96,3,192]{2,0,1:T(8,128)}, ...), condition=%wide.region_41.43_spmd.clone.clone, body=%wide.region_0.42_spmd.clone.clone.sunk | while | flops 26897362944 | bytes 1096088704 | solution.py:277
  21.7 35.5 %all_gather.38 = bf16[768,3,192]{2,1,0:T(4,128)(2,1)S(1)} all-gather(bf16[96,3,192]{2,1,0:T(4,128)(2,1)} %get-tuple-element.924), channel_id=1, replica_groups=mesh['dp'=2,'row'=4,'col'=4] {'dp','row'}, dimensions={0}, use_global_device_ids=true | all-gather | bytes 995328 | tf_op jit(solution)/shard_map/while/body/eval_jaxpr/all_gather | solution.py:171
  59.5 24.1 %all_gather.39 = bf16[768,192]{1,0:T(8,128)(2,1)S(1)} all-gather(bf16[96,192]{1,0:T(8,128)(2,1)S(1)} %copy-done.52), channel_id=1, replica_groups=mesh['dp'=2,'row'=4,'col'=4] {'dp','row'}, dimensions={0}, use_global_device_ids=true | all-gather | bytes 331776 | tf_op jit(solution)/shard_map/while/body/eval_jaxpr/all_gather | solution.py:172
  131.1 106.2 %reduce-scatter.9.cloned.1.call-done = f32[2048,192]{0,1:T(8,128)} async-done(((f32[2048,768]{0,1:T(8,128)}), f32[2048,192]{0,1:T(8,128)}) %reduce-scatter.9.cloned.1.call-update) | async-done | bytes 1572880 | tf_op jit(solution)/shard_map/while/body/eval_jaxpr/reduce_scatter | solution.py:190
  239.1 14.5 all-reduce.9
  256.2 7.9 all-gather.13.cloned.1.call-done
  264.1 64.9 %all-gather.11.cloned.1.call-done = bf16[2048,768]{0,1:T(8,128)(2,1)} async-done(((bf16[2048,192]{0,1:T(8,128)(2,1)}), bf16[2048,768]{0,1:T(8,128)(2,1)}) %all-gather.11.cloned.1.call-update) | async-done | bytes 3145744 | tf_op jit(solution)/shard_map/while/body/eval_jaxpr/all_gather | solution.py:195
  329.0 19.3 multiply_convert_fusion.7
  362.0 109.8 %reduce-scatter.11.cloned.1.call-done = f32[2048,192]{0,1:T(8,128)} async-done(((f32[2048,768]{0,1:T(8,128)}), f32[2048,192]{0,1:T(8,128)}) %reduce-scatter.11.cloned.1.call-update) | async-done | bytes 1572880 | tf_op jit(solution)/shard_map/while/body/eval_jaxpr/reduce_scatter | solution.py:198
  474.5 15.8 all-reduce.10
  493.8 13.2 all-reduce.11
  510.6 11.0 collective-permute-done
  523.0 68.3 %collective-permute-done.1 = bf16[2048,384]{0,1:T(8,128)(2,1)} collective-permute-done((bf16[2048,384]{0,1:T(8,128)(2,1)}, bf16[2048,384]{0,1:T(8,128)(2,1)}, u32[]{:S(2)}, u32[]{:S(2)}) %collective-permute-start.1) | collective-permute-done | bytes 1572896 | tf_op jit(solution)/shard_map/while/body/eval_jaxpr/ppermute | solution.py:19
  591.3 8.8 fusion.262
  600.1 9.6 fusion.263
  622.9 109.9 %reduce-scatter.13.cloned.1.call-done = f32[2048,192]{0,1:T(8,128)} async-done(((f32[2048,768]{0,1:T(8,128)}), f32[2048,192]{0,1:T(8,128)}) %reduce-scatter.13.cloned.1.call-update) | async-done | bytes 1572880 | tf_op jit(solution)/shard_map/while/body/eval_jaxpr/reduce_scatter | solution.py:48
  737.7 15.0 all-reduce.12
  756.8 14.7 collective-permute-done.2
  777.5 64.7 %collective-permute-done.3 = bf16[2048,384]{0,1:T(8,128)(2,1)} collective-permute-done((bf16[2048,384]{0,1:T(8,128)(2,1)S(1)}, bf16[2048,384]{0,1:T(8,128)(2,1)}, u32[]{:S(2)}, u32[]{:S(2)}) %collective-permute-start.3) | collective-permute-done | bytes 1572896 | tf_op jit(solution)/shard_map/while/body/eval_jaxpr/ppermute | solution.py:19
  842.2 10.7 fusion.267
  862.5 9.2 multiply_reduce_fusion.13
  883.6 9.6 multiply_convert_fusion.9
  951.4 8.2 reduce-scatter.17.cloned.1.call-done
  960.6 45.7 %reduce-scatter.15.cloned.1.call-done = f32[96,3,192]{2,0,1:T(8,128)} async-done(((f32[768,3,192]{2,0,1:T(8,128)}), f32[96,3,192]{2,0,1:T(8,128)}) %reduce-scatter.15.cloned.1.call-update) | async-done | bytes 221200 | tf_op jit(solution)/shard_map/while/body/eval_jaxpr/reduce_scatter | solution.py:252
  1008.0 111.3 %reduce-scatter.23.cloned.1.call-done = f32[2048,192]{0,1:T(8,128)} async-done(((f32[2048,768]{0,1:T(8,128)}), f32[2048,192]{0,1:T(8,128)}) %reduce-scatter.23.cloned.1.call-update) | async-done | bytes 1572880 | tf_op jit(solution)/shard_map/while/body/eval_jaxpr/reduce_scatter | solution.py:48
  1124.6 34.6 %all_gather.38 = bf16[768,3,192]{2,1,0:T(4,128)(2,1)S(1)} all-gather(bf16[96,3,192]{2,1,0:T(4,128)(2,1)} %get-tuple-element.924), channel_id=1, replica_groups=mesh['dp'=2,'row'=4,'col'=4] {'dp','row'}, dimensions={0}, use_global_device_ids=true | all-gather | bytes 995328 | tf_op jit(solution)/shard_map/while/body/eval_jaxpr/all_gather | solution.py:171
  1161.4 24.2 %all_gather.39 = bf16[768,192]{1,0:T(8,128)(2,1)S(1)} all-gather(bf16[96,192]{1,0:T(8,128)(2,1)S(1)} %copy-done.52), channel_id=1, replica_groups=mesh['dp'=2,'row'=4,'col'=4] {'dp','row'}, dimensions={0}, use_global_device_ids=true | all-gather | bytes 331776 | tf_op jit(solution)/shard_map/while/body/eval_jaxpr/all_gather | solution.py:172
  1231.9 106.4 %reduce-scatter.9.cloned.1.call-done = f32[2048,192]{0,1:T(8,128)} async-done(((f32[2048,768]{0,1:T(8,128)}), f32[2048,192]{0,1:T(8,128)}) %reduce-scatter.9.cloned.1.call-update) | async-done | bytes 1572880 | tf_op jit(solution)/shard_map/while/body/eval_jaxpr/reduce_scatter | solution.py:190
  1340.1 14.5 all-reduce.9
  1364.9 64.9 %all-gather.11.cloned.1.call-done = bf16[2048,768]{0,1:T(8,128)(2,1)} async-done(((bf16[2048,192]{0,1:T(8,128)(2,1)}), bf16[2048,768]{0,1:T(8,128)(2,1)}) %all-gather.11.cloned.1.call-update) | async-done | bytes 3145744 | tf_op jit(solution)/shard_map/while/body/eval_jaxpr/all_gather | solution.py:195
  1429.8 19.3 multiply_convert_fusion.7
  1462.8 109.8 %reduce-scatter.11.cloned.1.call-done = f32[2048,192]{0,1:T(8,128)} async-done(((f32[2048,768]{0,1:T(8,128)}), f32[2048,192]{0,1:T(8,128)}) %reduce-scatter.11.cloned.1.call-update) | async-done | bytes 1572880 | tf_op jit(solution)/shard_map/while/body/eval_jaxpr/reduce_scatter | solution.py:198
  1575.3 16.1 all-reduce.10
  1594.9 13.2 all-reduce.11
  1611.6 11.0 collective-permute-done
  1624.0 68.3 %collective-permute-done.1 = bf16[2048,384]{0,1:T(8,128)(2,1)} collective-permute-done((bf16[2048,384]{0,1:T(8,128)(2,1)}, bf16[2048,384]{0,1:T(8,128)(2,1)}, u32[]{:S(2)}, u32[]{:S(2)}) %collective-permute-start.1) | collective-permute-done | bytes 1572896 | tf_op jit(solution)/shard_map/while/body/eval_jaxpr/ppermute | solution.py:19
  1692.3 8.8 fusion.262
  1701.1 9.6 fusion.263
  1723.9 109.9 %reduce-scatter.13.cloned.1.call-done = f32[2048,192]{0,1:T(8,128)} async-done(((f32[2048,768]{0,1:T(8,128)}), f32[2048,192]{0,1:T(8,128)}) %reduce-scatter.13.cloned.1.call-update) | async-done | bytes 1572880 | tf_op jit(solution)/shard_map/while/body/eval_jaxpr/reduce_scatter | solution.py:48
  1838.8 15.1 all-reduce.12
  1857.8 14.6 collective-permute-done.2
  1878.2 64.7 %collective-permute-done.3 = bf16[2048,384]{0,1:T(8,128)(2,1)} collective-permute-done((bf16[2048,384]{0,1:T(8,128)(2,1)S(1)}, bf16[2048,384]{0,1:T(8,128)(2,1)}, u32[]{:S(2)}, u32[]{:S(2)}) %collective-permute-start.3) | collective-permute-done | bytes 1572896 | tf_op jit(solution)/shard_map/while/body/eval_jaxpr/ppermute | solution.py:19
  1943.0 10.7 fusion.267
  1963.3 9.2 multiply_reduce_fusion.13
  1984.4 9.6 multiply_convert_fusion.9
  2061.9 45.7 %reduce-scatter.15.cloned.1.call-done = f32[96,3,192]{2,0,1:T(8,128)} async-done(((f32[768,3,192]{2,0,1:T(8,128)}), f32[96,3,192]{2,0,1:T(8,128)}) %reduce-scatter.15.cloned.1.call-update) | async-done | bytes 221200 | tf_op jit(solution)/shard_map/while/body/eval_jaxpr/reduce_scatter | solution.py:252
  2109.4 111.3 %reduce-scatter.23.cloned.1.call-done = f32[2048,192]{0,1:T(8,128)} async-done(((f32[2048,768]{0,1:T(8,128)}), f32[2048,192]{0,1:T(8,128)}) %reduce-scatter.23.cloned.1.call-update) | async-done | bytes 1572880 | tf_op jit(solution)/shard_map/while/body/eval_jaxpr/reduce_scatter | solution.py:48
  2229.2 27.9 %all-reduce.4 = (f32[2,192]{1,0:T(2,128)}, f32[192]{0:T(256)}, f32[768]{0:T(1024)}, f32[192]{0:T(256)}, f32[2,192]{1,0:T(2,128)}, /*index=5*/f32[2,192]{1,0:T(2,128)}) all-reduce(f32[2,192]{1,0:T(2,128)S(1)} %copy-done.61, f32[192]{0:T(256)S(1)} %copy-done.63, ...), channel_id=1, replica_groups=mesh['dp'=2,'row'=4,'col'=4] {'dp','row'}, use_global_device_ids=true, to_apply=%region_42.44 | all-reduce | flops 2304 | bytes 18432 | tf_op jit(solution)/shard_map/psum | solution.py:279
  (575 shorter events, 420.3 us)
Async XLA Ops:
  19.7 68.3 %all-gather.9.cloned.1.call-start = ((), (), s32[]{:S(2)}) async-start(), calls=%async_computation.8 | async-start | bytes 3932160 | tf_op jit(solution)/shard_map/while/body/eval_jaxpr/all_gather | solution.py:181
  20.7 216.5 %reduce-scatter.9.cloned.1.call-start = ((), (), s32[]{:S(2)}) async-start(), calls=%async_computation.9 | async-start | bytes 7864320 | tf_op jit(solution)/shard_map/while/body/eval_jaxpr/reduce_scatter | solution.py:190
  127.6 109.7 %copy-start.25 = (bf16[2,192,2048]{2,1,0:T(8,128)(2,1)S(1)}, bf16[2,192,2048]{2,1,0:T(8,128)(2,1)}, u32[]{:S(2)}) copy-start(bf16[2,192,2048]{2,1,0:T(8,128)(2,1)} %copy-done.24) | copy-start | bytes 4718596 | tf_op jit(solution)/shard_map/while
  127.6 136.5 %all-gather.13.cloned.1.call-start = ((), (), s32[]{:S(2)}) async-start(), calls=%async_computation.11 | async-start | bytes 1327104 | tf_op jit(solution)/shard_map/while/body/eval_jaxpr/all_gather | solution.py:173
  128.3 200.6 %all-gather.11.cloned.1.call-start = ((), (), s32[]{:S(2)}) async-start(), calls=%async_computation.10 | async-start | bytes 3932160 | tf_op jit(solution)/shard_map/while/body/eval_jaxpr/all_gather | solution.py:195
  253.6 94.7 %copy-start.38 = (f32[2048]{0:T(1024)}, f32[2048]{0:T(1024)S(1)}, u32[]{:S(2)}) copy-start(f32[2048]{0:T(1024)S(1)} %get-tuple-element.796) | copy-start | bytes 24580 | tf_op jit(solution)/shard_map/while
  253.6 218.3 %copy-start.37 = (f32[2048]{0:T(1024)}, f32[2048]{0:T(1024)S(1)}, u32[]{:S(2)}) copy-start(f32[2048]{0:T(1024)S(1)} %get-tuple-element.797) | copy-start | bytes 24580 | tf_op jit(solution)/shard_map/while
  255.5 98.3 %all-gather.15.cloned.1.call-start = ((), (), s32[]{:S(2)}) async-start(), calls=%async_computation.12 | async-start | bytes 1327104 | tf_op jit(solution)/shard_map/while/body/eval_jaxpr/all_gather | solution.py:174
  256.1 215.7 %reduce-scatter.11.cloned.1.call-start = ((), (), s32[]{:S(2)}) async-start(), calls=%async_computation.13 | async-start | bytes 7864320 | tf_op jit(solution)/shard_map/while/body/eval_jaxpr/reduce_scatter | solution.py:198
  361.3 371.5 %reduce-scatter.13.cloned.1.call-start = ((), (), s32[]{:S(2)}) async-start(), calls=%async_computation.14 | async-start | bytes 7864320 | tf_op jit(solution)/shard_map/while/body/eval_jaxpr/reduce_scatter | solution.py:48
  474.5 258.4 %copy-start.4 = (f32[2048,192]{0,1:T(8,128)}, f32[2048,192]{0,1:T(8,128)S(1)}, u32[]{:S(2)}) copy-start(f32[2048,192]{0,1:T(8,128)S(1)} %get-tuple-element.799) | copy-start | bytes 4718596 | tf_op jit(solution)/shard_map/while
  510.1 11.4 collective-permute-start
  523.0 68.3 %collective-permute-start.1 = (bf16[2048,384]{0,1:T(8,128)(2,1)}, bf16[2048,384]{0,1:T(8,128)(2,1)}, u32[]{:S(2)}, u32[]{:S(2)}) collective-permute-start(bf16[2048,384]{0,1:T(8,128)(2,1)} %pad_maximum_fusion.9), channel_id=1, source_target_pairs={{0,2},{1,3},{2,0},{3,1},{4,6},{5,7},{6,4},{7,5},{8,10},{9,11},{10,... | collective-permute-start | bytes 4718600 | tf_op jit(solution)/shard_map/while/body/eval_jaxpr/ppermute | solution.py:19
  615.9 326.6 %reduce-scatter.19.cloned.1.call-start = ((), (), s32[]{:S(2)}) async-start(), calls=%async_computation.17 | async-start | bytes 2654208 | tf_op jit(solution)/shard_map/while/body/eval_jaxpr/reduce_scatter | solution.py:254
  622.9 321.4 %reduce-scatter.21.cloned.1.call-start = ((), (), s32[]{:S(2)}) async-start(), calls=%async_computation.18 | async-start | bytes 2654208 | tf_op jit(solution)/shard_map/while/body/eval_jaxpr/reduce_scatter | solution.py:255
  756.7 14.8 collective-permute-start.2
  771.7 70.5 %collective-permute-start.3 = (bf16[2048,384]{0,1:T(8,128)(2,1)S(1)}, bf16[2048,384]{0,1:T(8,128)(2,1)}, u32[]{:S(2)}, u32[]{:S(2)}) collective-permute-start(bf16[2048,384]{0,1:T(8,128)(2,1)S(1)} %pad_maximum_fusion.10), channel_id=1, source_target_pairs={{0,2},{1,3},{2,0},{3,1},{4,6},{5,7},{6,4},{7,5},{8,10},{9,11},{10,... | collective-permute-start | bytes 4718600 | tf_op jit(solution)/shard_map/while/body/eval_jaxpr/ppermute | solution.py:19
  777.1 182.5 %reduce-scatter.17.cloned.1.call-start = ((), (), s32[]{:S(2)}) async-start(), calls=%async_computation.16 | async-start | bytes 884736 | tf_op jit(solution)/shard_map/while/body/eval_jaxpr/reduce_scatter | solution.py:253
  924.1 82.2 %reduce-scatter.15.cloned.1.call-start = ((), (), s32[]{:S(2)}) async-start(), calls=%async_computation.15 | async-start | bytes 2654208 | tf_op jit(solution)/shard_map/while/body/eval_jaxpr/reduce_scatter | solution.py:252
  932.8 186.5 %reduce-scatter.23.cloned.1.call-start = ((), (), s32[]{:S(2)}) async-start(), calls=%async_computation.19 | async-start | bytes 7864320 | tf_op jit(solution)/shard_map/while/body/eval_jaxpr/reduce_scatter | solution.py:48
  939.6 179.7 %copy-start.7 = (f32[2048,192]{0,1:T(8,128)S(1)}, f32[2048,192]{0,1:T(8,128)}, u32[]{:S(2)}) copy-start(f32[2048,192]{0,1:T(8,128)} %copy-done.6) | copy-start | bytes 4718596 | tf_op jit(solution)/shard_map/while
  945.3 176.8 %copy-start.31 = (f32[96,768]{1,0:T(8,128)}, f32[96,768]{1,0:T(8,128)S(1)}, u32[]{:S(2)}) copy-start(f32[96,768]{1,0:T(8,128)S(1)} %select_add_fusion.17) | copy-start | bytes 884740 | tf_op jit(solution)/shard_map/while
  950.6 171.5 %copy-start.26 = (bf16[2,192,2048]{2,1,0:T(8,128)(2,1)S(1)}, bf16[2,192,2048]{2,1,0:T(8,128)(2,1)}, u32[]{:S(2)}) copy-start(bf16[2,192,2048]{2,1,0:T(8,128)(2,1)} %copy-done.24) | copy-start | bytes 4718596 | tf_op jit(solution)/shard_map/while
  960.6 161.5 %copy-start.41 = (f32[96,192]{1,0:T(8,128)}, f32[96,192]{1,0:T(8,128)S(1)}, u32[]{:S(2)}) copy-start(f32[96,192]{1,0:T(8,128)S(1)} %select_add_fusion.15) | copy-start | bytes 221188 | tf_op jit(solution)/shard_map/while
  1122.5 66.8 %all-gather.9.cloned.1.call-start = ((), (), s32[]{:S(2)}) async-start(), calls=%async_computation.8 | async-start | bytes 3932160 | tf_op jit(solution)/shard_map/while/body/eval_jaxpr/all_gather | solution.py:181
  1123.6 214.7 %reduce-scatter.9.cloned.1.call-start = ((), (), s32[]{:S(2)}) async-start(), calls=%async_computation.9 | async-start | bytes 7864320 | tf_op jit(solution)/shard_map/while/body/eval_jaxpr/reduce_scatter | solution.py:190
  1228.5 109.7 %copy-start.25 = (bf16[2,192,2048]{2,1,0:T(8,128)(2,1)S(1)}, bf16[2,192,2048]{2,1,0:T(8,128)(2,1)}, u32[]{:S(2)}) copy-start(bf16[2,192,2048]{2,1,0:T(8,128)(2,1)} %copy-done.24) | copy-start | bytes 4718596 | tf_op jit(solution)/shard_map/while
  1228.6 136.3 %all-gather.13.cloned.1.call-start = ((), (), s32[]{:S(2)}) async-start(), calls=%async_computation.11 | async-start | bytes 1327104 | tf_op jit(solution)/shard_map/while/body/eval_jaxpr/all_gather | solution.py:173
  1229.2 200.6 %all-gather.11.cloned.1.call-start = ((), (), s32[]{:S(2)}) async-start(), calls=%async_computation.10 | async-start | bytes 3932160 | tf_op jit(solution)/shard_map/while/body/eval_jaxpr/all_gather | solution.py:195
  1354.5 94.5 %copy-start.38 = (f32[2048]{0:T(1024)}, f32[2048]{0:T(1024)S(1)}, u32[]{:S(2)}) copy-start(f32[2048]{0:T(1024)S(1)} %get-tuple-element.796) | copy-start | bytes 24580 | tf_op jit(solution)/shard_map/while
  1354.6 218.1 %copy-start.37 = (f32[2048]{0:T(1024)}, f32[2048]{0:T(1024)S(1)}, u32[]{:S(2)}) copy-start(f32[2048]{0:T(1024)S(1)} %get-tuple-element.797) | copy-start | bytes 24580 | tf_op jit(solution)/shard_map/while
  1356.5 98.2 %all-gather.15.cloned.1.call-start = ((), (), s32[]{:S(2)}) async-start(), calls=%async_computation.12 | async-start | bytes 1327104 | tf_op jit(solution)/shard_map/while/body/eval_jaxpr/all_gather | solution.py:174
  1357.1 215.6 %reduce-scatter.11.cloned.1.call-start = ((), (), s32[]{:S(2)}) async-start(), calls=%async_computation.13 | async-start | bytes 7864320 | tf_op jit(solution)/shard_map/while/body/eval_jaxpr/reduce_scatter | solution.py:198
  1462.2 371.7 %reduce-scatter.13.cloned.1.call-start = ((), (), s32[]{:S(2)}) async-start(), calls=%async_computation.14 | async-start | bytes 7864320 | tf_op jit(solution)/shard_map/while/body/eval_jaxpr/reduce_scatter | solution.py:48
  1575.3 258.6 %copy-start.4 = (f32[2048,192]{0,1:T(8,128)}, f32[2048,192]{0,1:T(8,128)S(1)}, u32[]{:S(2)}) copy-start(f32[2048,192]{0,1:T(8,128)S(1)} %get-tuple-element.799) | copy-start | bytes 4718596 | tf_op jit(solution)/shard_map/while
  1611.1 11.4 collective-permute-start
  1624.0 68.3 %collective-permute-start.1 = (bf16[2048,384]{0,1:T(8,128)(2,1)}, bf16[2048,384]{0,1:T(8,128)(2,1)}, u32[]{:S(2)}, u32[]{:S(2)}) collective-permute-start(bf16[2048,384]{0,1:T(8,128)(2,1)} %pad_maximum_fusion.9), channel_id=1, source_target_pairs={{0,2},{1,3},{2,0},{3,1},{4,6},{5,7},{6,4},{7,5},{8,10},{9,11},{10,... | collective-permute-start | bytes 4718600 | tf_op jit(solution)/shard_map/while/body/eval_jaxpr/ppermute | solution.py:19
  1716.9 326.6 %reduce-scatter.19.cloned.1.call-start = ((), (), s32[]{:S(2)}) async-start(), calls=%async_computation.17 | async-start | bytes 2654208 | tf_op jit(solution)/shard_map/while/body/eval_jaxpr/reduce_scatter | solution.py:254
  1723.9 321.4 %reduce-scatter.21.cloned.1.call-start = ((), (), s32[]{:S(2)}) async-start(), calls=%async_computation.18 | async-start | bytes 2654208 | tf_op jit(solution)/shard_map/while/body/eval_jaxpr/reduce_scatter | solution.py:255
  1857.8 14.7 collective-permute-start.2
  1872.6 70.4 %collective-permute-start.3 = (bf16[2048,384]{0,1:T(8,128)(2,1)S(1)}, bf16[2048,384]{0,1:T(8,128)(2,1)}, u32[]{:S(2)}, u32[]{:S(2)}) collective-permute-start(bf16[2048,384]{0,1:T(8,128)(2,1)S(1)} %pad_maximum_fusion.10), channel_id=1, source_target_pairs={{0,2},{1,3},{2,0},{3,1},{4,6},{5,7},{6,4},{7,5},{8,10},{9,11},{10,... | collective-permute-start | bytes 4718600 | tf_op jit(solution)/shard_map/while/body/eval_jaxpr/ppermute | solution.py:19
  1878.0 182.9 %reduce-scatter.17.cloned.1.call-start = ((), (), s32[]{:S(2)}) async-start(), calls=%async_computation.16 | async-start | bytes 884736 | tf_op jit(solution)/shard_map/while/body/eval_jaxpr/reduce_scatter | solution.py:253
  2025.1 82.5 %reduce-scatter.15.cloned.1.call-start = ((), (), s32[]{:S(2)}) async-start(), calls=%async_computation.15 | async-start | bytes 2654208 | tf_op jit(solution)/shard_map/while/body/eval_jaxpr/reduce_scatter | solution.py:252
  2033.8 186.9 %reduce-scatter.23.cloned.1.call-start = ((), (), s32[]{:S(2)}) async-start(), calls=%async_computation.19 | async-start | bytes 7864320 | tf_op jit(solution)/shard_map/while/body/eval_jaxpr/reduce_scatter | solution.py:48
  2040.6 180.0 %copy-start.7 = (f32[2048,192]{0,1:T(8,128)S(1)}, f32[2048,192]{0,1:T(8,128)}, u32[]{:S(2)}) copy-start(f32[2048,192]{0,1:T(8,128)} %copy-done.6) | copy-start | bytes 4718596 | tf_op jit(solution)/shard_map/while
  2046.4 177.0 %copy-start.31 = (f32[96,768]{1,0:T(8,128)}, f32[96,768]{1,0:T(8,128)S(1)}, u32[]{:S(2)}) copy-start(f32[96,768]{1,0:T(8,128)S(1)} %select_add_fusion.17) | copy-start | bytes 884740 | tf_op jit(solution)/shard_map/while
  2051.8 171.6 %copy-start.26 = (bf16[2,192,2048]{2,1,0:T(8,128)(2,1)S(1)}, bf16[2,192,2048]{2,1,0:T(8,128)(2,1)}, u32[]{:S(2)}) copy-start(bf16[2,192,2048]{2,1,0:T(8,128)(2,1)} %copy-done.24) | copy-start | bytes 4718596 | tf_op jit(solution)/shard_map/while
  2061.9 161.6 %copy-start.41 = (f32[96,192]{1,0:T(8,128)}, f32[96,192]{1,0:T(8,128)S(1)}, u32[]{:S(2)}) copy-start(f32[96,192]{1,0:T(8,128)S(1)} %select_add_fusion.15) | copy-start | bytes 221188 | tf_op jit(solution)/shard_map/while
  (133 other events, 1544.8 us)
Sparse Core Ops, SparseCore 0:
  22.6 65.3 all-gather.8
  127.7 109.5 reduce-scatter.8
  239.2 24.8 all-gather.12
  266.1 62.8 all-gather.10
  330.7 23.1 all-gather.14
  361.5 110.3 reduce-scatter.10
  616.0 116.7 reduce-scatter.12
  736.2 42.7 reduce-scatter.18
  782.3 43.9 reduce-scatter.20
  924.2 35.3 reduce-scatter.16
  963.6 42.7 reduce-scatter.14
  1008.5 110.8 reduce-scatter.22
  1125.5 63.8 all-gather.8
  1228.7 109.5 reduce-scatter.8
  1340.0 24.8 all-gather.12
  1366.9 62.8 all-gather.10
  1431.5 23.1 all-gather.14
  1462.3 110.3 reduce-scatter.10
  1717.0 116.7 reduce-scatter.12
  1837.1 42.7 reduce-scatter.18
  1883.2 44.0 reduce-scatter.20
  2025.2 35.6 reduce-scatter.16
  2064.9 42.6 reduce-scatter.14
  2109.7 110.8 reduce-scatter.22
